TPU v7x, 32 devices: a whole 2x2x4 slice. The times are simulated.
32 devices in a mesh: dp: 8 (over z, x), ctx: 4 (over y, core).
Axes of the slice: x: 2, y: 2, z: 4, core: 2. Of those that a mesh axis runs over, the one named last changes fastest.
Arguments:
- states: bfloat16 [32, 1024, 960], P('dp', 'ctx'), may hold values from -6 to 6
- teacher: bfloat16 [32, 1024, 960], P('dp', 'ctx'), may hold values from -6 to 6
- validity: int32 [32, 1024], P('dp', 'ctx'), may hold values from 0 to 1, as said below
- chosen: int32 [32, 1024], P('dp', 'ctx'), may hold values from 0 to 1, as said below
- attn_pack: bfloat16 [960, 2560], P(None, ('dp', 'ctx')), may hold values from -1 to 1
- gate_up: bfloat16 [960, 5120], P(None, ('dp', 'ctx')), may hold values from -0.1875 to 0.1875
- down_proj: bfloat16 [960, 2560], P(None, ('dp', 'ctx')), may hold values from -0.125 to 0.125
- norm_gains: float32 [2, 960], replicated, may hold values from 0.25 to 1.75
- router: float32 [960], replicated, may hold values from -0.12 to 0.12
Outputs:
- states_out: bfloat16 [32, 1024, 960], P('dp', 'ctx')
- mse_loss: float32 [], replicated
- states_grad: float32 [32, 1024, 960], P('dp', 'ctx')
- attn_pack_grad: float32 [960, 2560], P(None, ('dp', 'ctx'))
- gate_up_grad: float32 [960, 5120], P(None, ('dp', 'ctx'))
- down_proj_grad: float32 [960, 2560], P(None, ('dp', 'ctx'))
- norm_gains_grad: float32 [2, 960], replicated
- router_grad: float32 [960], replicated
Inputs may be any that keep to these rules, and one draw needn't show every extreme that they name: `validity`: the first token of every sequence is valid. `chosen`: each sequence has 640 or 641 selected tokens, the first token always among them.
All inputs are finite; a program needn't handle non-finite values.
Results may differ from a plain program's by a relative error of at most 0.012.
Values may be sent and summed in bfloat16 or wider, within the bound.
No kernel may reach another device: no remote copies, remote signals or barrier semaphores. Data moves between devices by JAX's collectives and lax.ppermute only.
A program may use at most 320 MiB of HBM per device.

v0:
```python
import jax
import jax.numpy as jnp
from jax import lax
from jax.sharding import PartitionSpec as P

D = 960
HEADS = 15
KV_HEADS = 5
HEAD = 64
FF = 2560
MICRO = 2
EPS = 1e-05
THETA = 10000.0


def shortened(x):
    return jax.tree.map(lambda a: a.astype(jnp.bfloat16) if a.dtype == jnp.float32 else a, x)


def rope_tables(positions):
    half_head = HEAD // 2
    freqs = THETA ** (-(jnp.arange(half_head).astype(jnp.float32) * 2.0 / HEAD))
    angles = positions.astype(jnp.float32)[:, None] * freqs[None, :]
    return (jnp.cos(angles)[:, None, :], jnp.sin(angles)[:, None, :])


def rotate(values, cosine, sine):
    half_head = HEAD // 2
    first = values[..., :half_head]
    second = values[..., half_head:]
    return jnp.concatenate(
        [first * cosine - second * sine, second * cosine + first * sine], axis=-1
    )


def rotate_back(values, cosine, sine):
    half_head = HEAD // 2
    first = values[..., :half_head]
    second = values[..., half_head:]
    return jnp.concatenate(
        [first * cosine + second * sine, second * cosine - first * sine], axis=-1
    )


def norm_back(grad_out, values, inv_rms, gain_row):
    scaled = grad_out * gain_row
    return inv_rms * scaled - values * inv_rms**3 * jnp.mean(
        scaled * values, axis=-1, keepdims=True
    )


def scores_of(queries, keys, allowed):
    scores = (
        jnp.einsum("bqgrh,bkgh->bgrqk", queries, keys, preferred_element_type=jnp.float32) * 0.125
    )
    return jnp.where(allowed, scores, -jnp.inf)


def over_rows(left, right):
    return lax.dot_general(
        left, right, (((0, 1), (0, 1)), ((), ())), preferred_element_type=jnp.float32
    )


def by_columns(left, right):
    return lax.dot_general(
        left, right, (((2,), (1,)), ((), ())), preferred_element_type=jnp.float32
    )


def on_device(states, teacher, validity, chosen, attn_pack, gate_up, down_proj, norm_gains, router):
    seq_count, block_rows, width = states.shape
    seq_micro = seq_count // MICRO
    ctx_count = lax.axis_size("ctx")
    dp_count = lax.axis_size("dp")
    ctx_spot = lax.axis_index("ctx")
    seq_length = block_rows * ctx_count
    qkv_cols = D + 2 * KV_HEADS * HEAD
    kv_width = KV_HEADS * HEAD
    per_kv = HEADS // KV_HEADS
    cosine, sine = rope_tables(ctx_spot * block_rows + jnp.arange(block_rows))
    early_block = jnp.arange(seq_length) // block_rows <= ctx_spot
    valid_all = validity.astype(jnp.float32)
    chosen_all = chosen.astype(jnp.float32)
    key_flags = (validity * chosen).astype(jnp.bfloat16)
    gain_one = norm_gains[0]
    gain_two = norm_gains[1]
    packs = (attn_pack, gate_up, down_proj)
    valid_total = lax.psum(jnp.sum(valid_all), ("dp", "ctx"))
    grad_attn = jnp.zeros((D, qkv_cols + D), jnp.float32)
    grad_gu = jnp.zeros((D, 2 * FF), jnp.float32)
    grad_down = jnp.zeros((D, FF), jnp.float32)
    grad_gain_one = jnp.zeros((D,), jnp.float32)
    grad_gain_two = jnp.zeros((D,), jnp.float32)
    grad_router = jnp.zeros((D,), jnp.float32)
    energy = jnp.zeros((), jnp.float32)
    out_parts = []
    input_grads = []
    for micro_index in range(MICRO):
        lower = micro_index * seq_micro
        upper = lower + seq_micro
        x_float = states[lower:upper].astype(jnp.float32)
        teacher_rows = teacher[lower:upper].astype(jnp.float32)
        valid_rows = valid_all[lower:upper]
        chosen_rows = chosen_all[lower:upper]
        fresh = (
            lax.all_gather(packs[0], ("dp", "ctx"), axis=1, tiled=True),
            lax.all_gather(packs[1], ("dp", "ctx"), axis=1, tiled=True),
            lax.all_gather(packs[2], ("dp", "ctx"), axis=1, tiled=True),
        )
        w_attn, w_gu, w_down = fresh
        inv_one = lax.rsqrt(jnp.mean(x_float * x_float, axis=-1, keepdims=True) + EPS)
        normed = (x_float * inv_one * gain_one).astype(jnp.bfloat16)
        mixed = jnp.dot(normed, w_attn[:, :qkv_cols], preferred_element_type=jnp.float32)
        queries = mixed[..., :D].reshape(seq_micro, block_rows, HEADS, HEAD)
        keys = mixed[..., D : D + kv_width].reshape(seq_micro, block_rows, KV_HEADS, HEAD)
        values_in = mixed[..., D + kv_width :].reshape(seq_micro, block_rows, KV_HEADS, HEAD)
        rot_queries = (
            rotate(queries, cosine, sine)
            .astype(jnp.bfloat16)
            .reshape(seq_micro, block_rows, KV_HEADS, per_kv, HEAD)
        )
        rot_keys = rotate(keys, cosine, sine).astype(jnp.bfloat16)
        value_low = values_in.astype(jnp.bfloat16)
        keys_all, values_all, flags_all = (
            lax.all_gather(rot_keys, "ctx", axis=1, tiled=True),
            lax.all_gather(value_low, "ctx", axis=1, tiled=True),
            lax.all_gather(key_flags[lower:upper], "ctx", axis=1, tiled=True),
        )
        allowed = (early_block[None, :] & (flags_all > 0.5))[:, None, None, None, :]
        scores = scores_of(rot_queries, keys_all, allowed)
        row_max = jnp.max(scores, axis=-1, keepdims=True)
        expd = jnp.exp(scores - row_max)
        row_total = jnp.sum(expd, axis=-1, keepdims=True)
        log_total = row_max + jnp.log(row_total)
        probs_low = (expd / row_total).astype(jnp.bfloat16)
        heads_out = jnp.einsum(
            "bgrqk,bkgh->bqgrh", probs_low, values_all, preferred_element_type=jnp.float32
        )
        heads_low = heads_out.reshape(seq_micro, block_rows, D).astype(jnp.bfloat16)
        attn_out = by_columns(heads_low, w_attn[:, qkv_cols:])
        inner = x_float + attn_out
        inv_two = lax.rsqrt(jnp.mean(inner * inner, axis=-1, keepdims=True) + EPS)
        normed_two = (inner * inv_two * gain_two).astype(jnp.bfloat16)
        gate_both = jnp.dot(normed_two, w_gu, preferred_element_type=jnp.float32)
        gate_part = gate_both[..., :FF]
        up_part = gate_both[..., FF:]
        gate_sig = jax.nn.sigmoid(gate_part)
        hidden = (gate_part * gate_sig * up_part).astype(jnp.bfloat16)
        ffn_out = by_columns(hidden, w_down)
        gate_prob = jax.nn.sigmoid(jnp.dot(x_float, router, precision=lax.Precision.HIGHEST))
        weight_mix = chosen_rows * gate_prob
        branch = attn_out + ffn_out
        result = x_float + weight_mix[..., None] * branch
        out_parts.append(result.astype(jnp.bfloat16))
        diff = valid_rows[..., None] * (result - teacher_rows)
        energy = energy + 0.5 * jnp.sum(diff * diff)
        w_attn, w_gu, w_down = (
            lax.all_gather(packs[0], ("dp", "ctx"), axis=1, tiled=True),
            lax.all_gather(packs[1], ("dp", "ctx"), axis=1, tiled=True),
            lax.all_gather(packs[2], ("dp", "ctx"), axis=1, tiled=True),
        )
        d_branch = weight_mix[..., None] * diff
        d_logit = chosen_rows * jnp.sum(diff * branch, axis=-1) * gate_prob * (1.0 - gate_prob)
        grad_router = grad_router + jnp.einsum(
            "bt,btd->d", d_logit, x_float, precision=lax.Precision.HIGHEST
        )
        d_states = diff + d_logit[..., None] * router
        d_ffn = d_branch.astype(jnp.bfloat16)
        d_hidden = jnp.dot(d_ffn, w_down, preferred_element_type=jnp.float32)
        grad_down = grad_down + over_rows(d_ffn, hidden)
        d_gate = d_hidden * up_part * gate_sig * (1.0 + gate_part * (1.0 - gate_sig))
        d_up = d_hidden * gate_part * gate_sig
        d_gu_low = jnp.concatenate([d_gate, d_up], axis=-1).astype(jnp.bfloat16)
        d_normed_two = by_columns(d_gu_low, w_gu)
        grad_gu = grad_gu + over_rows(normed_two, d_gu_low)
        grad_gain_two = grad_gain_two + jnp.sum(d_normed_two * inner * inv_two, axis=(0, 1))
        d_inner = norm_back(d_normed_two, inner, inv_two, gain_two)
        d_states = d_states + d_inner
        d_attn_low = (d_branch + d_inner).astype(jnp.bfloat16)
        d_heads = jnp.dot(d_attn_low, w_attn[:, qkv_cols:], preferred_element_type=jnp.float32)
        d_heads_low = d_heads.astype(jnp.bfloat16).reshape(
            seq_micro, block_rows, KV_HEADS, per_kv, HEAD
        )
        grad_out_proj = over_rows(d_attn_low, heads_low)
        probs = jnp.exp(scores_of(rot_queries, keys_all, allowed) - log_total)
        d_probs = jnp.einsum(
            "bqgrh,bkgh->bgrqk", d_heads_low, values_all, preferred_element_type=jnp.float32
        )
        d_scores = (probs * (d_probs - jnp.sum(probs * d_probs, axis=-1, keepdims=True))).astype(
            jnp.bfloat16
        )
        d_queries = (
            jnp.einsum("bgrqk,bkgh->bqgrh", d_scores, keys_all, preferred_element_type=jnp.float32)
            * 0.125
        )
        d_keys_all = (
            jnp.einsum(
                "bgrqk,bqgrh->bkgh", d_scores, rot_queries, preferred_element_type=jnp.float32
            )
            * 0.125
        )
        d_values_all = jnp.einsum(
            "bgrqk,bqgrh->bkgh",
            probs.astype(jnp.bfloat16),
            d_heads_low,
            preferred_element_type=jnp.float32,
        )
        d_keys, d_values = (
            lax.psum_scatter(
                d_keys_all.astype(jnp.bfloat16), "ctx", scatter_dimension=1, tiled=True
            ).astype(jnp.float32),
            lax.psum_scatter(
                d_values_all.astype(jnp.bfloat16), "ctx", scatter_dimension=1, tiled=True
            ).astype(jnp.float32),
        )
        d_queries = rotate_back(d_queries.reshape(seq_micro, block_rows, HEADS, HEAD), cosine, sine)
        d_keys = rotate_back(d_keys, cosine, sine)
        d_mixed = jnp.concatenate(
            [
                d_queries.reshape(seq_micro, block_rows, D),
                d_keys.reshape(seq_micro, block_rows, kv_width),
                d_values.reshape(seq_micro, block_rows, kv_width),
            ],
            axis=-1,
        ).astype(jnp.bfloat16)
        d_normed = by_columns(d_mixed, w_attn[:, :qkv_cols])
        grad_attn = grad_attn + jnp.concatenate([over_rows(normed, d_mixed), grad_out_proj], axis=1)
        grad_gain_one = grad_gain_one + jnp.sum(d_normed * x_float * inv_one, axis=(0, 1))
        d_states = d_states + norm_back(d_normed, x_float, inv_one, gain_one)
        input_grads.append(d_states)

    def owner_layout(grad_whole):
        return grad_whole.reshape(
            D, dp_count, ctx_count, grad_whole.shape[1] // (dp_count * ctx_count)
        )

    by_ctx = (
        lax.all_to_all(
            owner_layout(grad_attn).astype(jnp.bfloat16),
            "ctx",
            split_axis=2,
            concat_axis=2,
            tiled=True,
        ).astype(jnp.float32),
        lax.all_to_all(
            owner_layout(grad_gu).astype(jnp.bfloat16),
            "ctx",
            split_axis=2,
            concat_axis=2,
            tiled=True,
        ).astype(jnp.float32),
        lax.all_to_all(
            owner_layout(grad_down).astype(jnp.bfloat16),
            "ctx",
            split_axis=2,
            concat_axis=2,
            tiled=True,
        ).astype(jnp.float32),
    )
    attn_ctx, gu_ctx, down_ctx = [jnp.sum(piece, axis=2) for piece in by_ctx]
    by_dp = (
        lax.all_to_all(shortened(attn_ctx), "dp", split_axis=1, concat_axis=1, tiled=True).astype(
            attn_ctx.dtype
        ),
        lax.all_to_all(shortened(gu_ctx), "dp", split_axis=1, concat_axis=1, tiled=True).astype(
            gu_ctx.dtype
        ),
        lax.all_to_all(shortened(down_ctx), "dp", split_axis=1, concat_axis=1, tiled=True).astype(
            down_ctx.dtype
        ),
    )
    attn_grad_part, gu_grad_part, down_grad_part = [jnp.sum(piece, axis=1) for piece in by_dp]
    grad_gains = jnp.stack([grad_gain_one, grad_gain_two], axis=0)
    energy_all, gains_all, router_all = lax.psum((energy, grad_gains, grad_router), ("dp", "ctx"))
    mse_loss = 2.0 * energy_all / (valid_total * D)
    return (
        jnp.concatenate(out_parts, axis=0),
        mse_loss,
        jnp.concatenate(input_grads, axis=0),
        attn_grad_part,
        gu_grad_part,
        down_grad_part,
        gains_all,
        router_all,
    )


def solution(mesh):
    placed = (
        P("dp", "ctx", None),
        P("dp", "ctx", None),
        P("dp", "ctx"),
        P("dp", "ctx"),
        P(None, ("dp", "ctx")),
        P(None, ("dp", "ctx")),
        P(None, ("dp", "ctx")),
        P(),
        P(),
    )
    return jax.shard_map(
        on_device,
        mesh=mesh,
        in_specs=placed,
        out_specs=(
            P("dp", "ctx", None),
            P(),
            P("dp", "ctx", None),
            P(None, ("dp", "ctx")),
            P(None, ("dp", "ctx")),
            P(None, ("dp", "ctx")),
            P(),
            P(),
        ),
        check_vma=False,
    )
```

profile of v0, /device:TPU:0, one launch (start us, length us, event | category | flops | bytes accessed | tf_op | source)
XLA Modules:
  0.0 1026.9 jit_solution(13568377429993740406)
XLA Ops:
  10.8 68.1 %all-gather.8.cloned.1.call-done = bf16[960,2560]{0,1:T(8,128)(2,1)} async-done(((bf16[960,80]{0,1:T(8,128)(2,1)}), bf16[960,2560]{0,1:T(8,128)(2,1)}) %all-gather.8.cloned.1.call-update) | async-done | bytes 4915216 | tf_op jit(solution)/shard_map/all_gather | solution.py:107
  110.5 15.0 %bitcast_reduce_fusion = (f32[2,5,3,256]{3,2,1,0:T(4,128)S(1)}, f32[2,5,1024,256,3]{3,2,4,1,0:T(8,128)}) fusion(bf16[2,256,5,3,32]{1,4,3,2,0:T(8,128)(2,1)S(1)} %bitcast.322, bf16[2,256,5,3,32]{1,4,3,2,0:T(8,128)(2,1)} %bitcast.324, bf16[2,1024,5,64]{1,3,2,0:T(8,128)(2,1)} %all-gather.20.cloned.1.call-done, pred[2,1024]{1,0:T(4,128)(4,1)S(1)} %get-tuple-element.98), kind=kOutput, calls=%fused_computation.12 | convolution fusion | flops 1032184320 | bytes 33783808 | tf_op jit(solution)/shard_map/bqgrh,bkgh->bgrqk/dot_general | solution.py:54
  125.5 13.0 %fusion.11 = f32[2,5,3,256]{3,2,1,0:T(4,128)S(1)} fusion(f32[2,5,1024,256,3]{3,2,4,1,0:T(8,128)} %get-tuple-element.100, f32[2,5,3,256]{3,2,1,0:T(4,128)S(1)} %get-tuple-element.99), kind=kLoop, calls=%fused_computation.25 | loop fusion | flops 15720960 | bytes 31518720 | tf_op jit(solution)/shard_map/reduce_sum | solution.py:134
  138.5 14.3 %bitcast_reduce_fusion.1 = (f32[2,5,3,256]{3,2,1,0:T(4,128)S(1)}, f32[2,5,1024,256,3]{3,2,4,1,0:T(8,128)}) fusion(bf16[2,256,5,3,32]{1,4,3,2,0:T(8,128)(2,1)S(1)} %bitcast.320, bf16[2,256,5,3,32]{1,4,3,2,0:T(8,128)(2,1)S(1)} %bitcast.318, bf16[2,1024,5,64]{1,3,2,0:T(8,128)(2,1)} %all-gather.12.cloned.1.call-done, pred[2,1024]{1,0:T(4,128)(4,1)S(1)} %get-tuple-element.97), kind=kOutput, calls=%fused_computation.17 | convolution fusion | flops 1032184320 | bytes 33783808 | tf_op jit(solution)/shard_map/bqgrh,bkgh->bgrqk/dot_general | solution.py:54
  152.8 13.1 %fusion.10 = f32[2,5,3,256]{3,2,1,0:T(4,128)S(1)} fusion(f32[2,5,1024,256,3]{3,2,4,1,0:T(8,128)} %get-tuple-element.102, f32[2,5,3,256]{3,2,1,0:T(4,128)S(1)} %get-tuple-element.101), kind=kLoop, calls=%fused_computation.24 | loop fusion | flops 15720960 | bytes 31518720 | tf_op jit(solution)/shard_map/reduce_sum | solution.py:134
  166.0 13.3 %fusion.72 = bf16[2,5,64,3,256]{4,2,3,1,0:T(8,128)(2,1)S(1)} fusion(f32[2,5,1024,256,3]{3,2,4,1,0:T(8,128)} %get-tuple-element.100, f32[2,5,3,256]{3,2,1,0:T(4,128)S(1)} %fusion.11, f32[2,5,3,256]{3,2,1,0:T(4,128)S(1)} %get-tuple-element.99, bf16[2,1024,5,64]{1,3,2,0:T(8,128)(2,1)} %all-gather.18.cloned.1.call-done), kind=kOutput, calls=%fused_computation.144 | convolution fusion | flops 1030717440 | bytes 33812480 | tf_op jit(solution)/shard_map/bgrqk,bkgh->bqgrh/dot_general | solution.py:137
  183.7 13.5 %fusion.73 = bf16[2,5,64,3,256]{4,2,3,1,0:T(8,128)(2,1)S(1)} fusion(f32[2,5,1024,256,3]{3,2,4,1,0:T(8,128)} %get-tuple-element.102, f32[2,5,3,256]{3,2,1,0:T(4,128)S(1)} %fusion.10, f32[2,5,3,256]{3,2,1,0:T(4,128)S(1)} %get-tuple-element.101, bf16[2,1024,5,64]{1,3,2,0:T(8,128)(2,1)} %all-gather.10.cloned.1.call-done), kind=kOutput, calls=%fused_computation.145 | convolution fusion | flops 1030717440 | bytes 33812480 | tf_op jit(solution)/shard_map/bgrqk,bkgh->bqgrh/dot_general | solution.py:137
  197.2 5.7 multiply_reduce_fusion.9
  203.7 50.6 %all-gather.14.cloned.1.call-done = bf16[960,5120]{0,1:T(8,128)(2,1)} async-done(((bf16[960,160]{0,1:T(8,128)(2,1)}), bf16[960,5120]{0,1:T(8,128)(2,1)}) %all-gather.14.cloned.1.call-update) | async-done | bytes 9830416 | tf_op jit(solution)/shard_map/all_gather | solution.py:108
  254.3 9.5 fusion.27
  268.8 8.9 fusion.29
  284.5 36.5 %all-gather.16.cloned.1.call-done = bf16[960,2560]{0,1:T(8,128)(2,1)} async-done(((bf16[960,80]{0,1:T(8,128)(2,1)}), bf16[960,2560]{0,1:T(8,128)(2,1)}) %all-gather.16.cloned.1.call-update) | async-done | bytes 4915216 | tf_op jit(solution)/shard_map/all_gather | solution.py:109
  321.0 8.0 fusion.66
  329.1 10.3 multiply_reduce_fusion.3
  339.4 11.5 %multiply_convert_fusion.3 = (bf16[2,256,2560]{2,1,0:T(8,128)(2,1)S(1)}, bf16[2,256,2560]{2,1,0:T(8,128)(2,1)}) fusion(f32[2,256,5120]{2,1,0:T(8,128)} %copy-done.6, bf16[960,2560]{0,1:T(8,128)(2,1)} %all-gather.16.cloned.1.call-done, f32[2,256,960]{1,2,0:T(8,128)S(1)} %get-tuple-element.43, f32[2,256]{1,0:T(2,128)S(1)} %copy-done.48), kind=kOutput, calls=%fused_computation.62 | convolution fusion | flops 2534604800 | bytes 22611968 | tf_op jit(solution)/shard_map/dot_general | solution.py:170
  350.9 10.2 multiply_convert_fusion.1
  361.1 13.9 %fusion.25 = f32[2,256,960]{1,2,0:T(8,128)} fusion(bf16[960,5120]{0,1:T(8,128)(2,1)} %all-gather.14.cloned.1.call-done, bf16[2,256,2560]{2,1,0:T(8,128)(2,1)} %get-tuple-element.37, bf16[2,256,2560]{2,1,0:T(8,128)(2,1)S(1)} %get-tuple-element.36), kind=kOutput, calls=%fused_computation.38 | convolution fusion | flops 5043650560 | bytes 17039360 | tf_op jit(solution)/shard_map/dot_general | solution.py:66
  375.0 15.0 %multiply_reduce_fusion = (f32[960]{0:T(1024)}, f32[2,256]{1,0:T(2,128)S(1)}, f32[2,256]{1,0:T(2,128)S(1)}, f32[960]{0:T(1024)}, f32[2,256,960]{1,2,0:T(8,128)}) fusion(f32[2,256,960]{1,2,0:T(8,128)} %get-tuple-element.53, f32[2,256]{1,0:T(2,128)S(1)} %get-tuple-element.90, f32[960]{0:T(1024)S(1)} %bitcast.340, f32[2,256,960]{1,2,0:T(8,128)} %get-tuple-element.31, ...), kind=kOutput, calls=%fused_computation.116 | convolution fusion | flops 5049545728 | bytes 22957312 | tf_op jit(solution)/shard_map/dot_general | solution.py:66
  390.0 5.9 add_convert_fusion
  399.2 24.1 %fusion = (f32[2,5,3,256]{3,2,1,0:T(4,128)S(1)}, f32[2,5,1024,256,3]{3,2,4,1,0:T(8,128)}) fusion(f32[2,5,1024,256,3]{3,2,4,1,0:T(8,128)} %get-tuple-element.100, f32[2,5,3,256]{3,2,1,0:T(4,128)S(1)} %log_add_fusion, bf16[2,256,5,3,64]{1,4,3,2,0:T(8,128)(2,1)S(1)} %bitcast.312, bf16[2,1024,5,64]{1,3,2,0:T(8,128)(2,1)S(1)} %copy-done.26), kind=kOutput, calls=%fused_computation.2 | convolution fusion | flops 1030218240 | bytes 65269760 | tf_op jit(solution)/shard_map/bqgrh,bkgh->bgrqk/dot_general | solution.py:187
  423.3 26.8 %fusion.2 = bf16[2,5,3,256,1024]{3,4,2,1,0:T(8,128)(2,1)} fusion(f32[2,5,1024,256,3]{3,2,4,1,0:T(8,128)} %get-tuple-element.106, f32[2,5,1024,256,3]{3,2,4,1,0:T(8,128)} %get-tuple-element.100, f32[2,5,3,256]{3,2,1,0:T(4,128)S(1)} %get-tuple-element.105, f32[2,5,3,256]{3,2,1,0:T(4,128)S(1)} %log_add_fusion), kind=kLoop, calls=%fused_computation.4 | loop fusion | flops 31457280 | bytes 78704640 | tf_op jit(solution)/shard_map/convert_element_type | solution.py:190
  450.1 11.4 %fusion.81 = bf16[2,1024,5,64]{1,3,2,0:T(8,128)(2,1)} fusion(bf16[2,5,3,256,1024]{3,4,2,1,0:T(8,128)(2,1)} %fusion.2, bf16[2,256,5,3,32]{1,4,3,2,0:T(8,128)(2,1)S(1)} %bitcast.323, bf16[2,256,5,3,32]{1,4,3,2,0:T(8,128)(2,1)S(1)} %bitcast.325), kind=kOutput, calls=%fused_computation.149 | convolution fusion | flops 1009909760 | bytes 18022400 | tf_op jit(solution)/shard_map/bgrqk,bqgrh->bkgh/dot_general | solution.py:198
  464.7 24.4 %fusion.3 = (f32[2,5,3,256]{3,2,1,0:T(4,128)S(1)}, f32[2,5,1024,256,3]{3,2,4,1,0:T(8,128)}) fusion(f32[2,5,1024,256,3]{3,2,4,1,0:T(8,128)} %get-tuple-element.102, f32[2,5,3,256]{3,2,1,0:T(4,128)S(1)} %copy-done.30, bf16[2,256,5,3,64]{1,4,3,2,0:T(8,128)(2,1)S(1)} %bitcast.310, bf16[2,1024,5,64]{1,3,2,0:T(8,128)(2,1)S(1)} %copy-done.25), kind=kOutput, calls=%fused_computation.7 | convolution fusion | flops 1030218240 | bytes 65269760 | tf_op jit(solution)/shard_map/bqgrh,bkgh->bgrqk/dot_general | solution.py:187
  489.1 26.6 %fusion.5 = bf16[2,5,3,256,1024]{3,4,2,1,0:T(8,128)(2,1)} fusion(f32[2,5,1024,256,3]{3,2,4,1,0:T(8,128)} %get-tuple-element.108, f32[2,5,1024,256,3]{3,2,4,1,0:T(8,128)} %get-tuple-element.102, f32[2,5,3,256]{3,2,1,0:T(4,128)S(1)} %get-tuple-element.107, f32[2,5,3,256]{3,2,1,0:T(4,128)S(1)} %copy-done.30), kind=kLoop, calls=%fused_computation.9 | loop fusion | flops 31457280 | bytes 78704640 | tf_op jit(solution)/shard_map/convert_element_type | solution.py:190
  515.7 11.5 %fusion.80 = bf16[2,1024,5,64]{1,3,2,0:T(8,128)(2,1)} fusion(bf16[2,5,3,256,1024]{3,4,2,1,0:T(8,128)(2,1)} %fusion.5, bf16[2,256,5,3,32]{1,4,3,2,0:T(8,128)(2,1)} %bitcast.321, bf16[2,256,5,3,32]{1,4,3,2,0:T(8,128)(2,1)S(1)} %bitcast.319), kind=kOutput, calls=%fused_computation.148 | convolution fusion | flops 1009909760 | bytes 18022400 | tf_op jit(solution)/shard_map/bgrqk,bqgrh->bkgh/dot_general | solution.py:198
  527.3 14.8 %fusion.77 = bf16[2,1024,5,64]{1,3,2,0:T(8,128)(2,1)} fusion(bf16[2,256,5,3,64]{1,4,3,2,0:T(8,128)(2,1)} %bitcast.313, f32[2,5,1024,256,3]{3,2,4,1,0:T(8,128)} %get-tuple-element.100, f32[2,5,3,256]{3,2,1,0:T(4,128)S(1)} %log_add_fusion), kind=kOutput, calls=%fused_computation.147 | convolution fusion | flops 1023016960 | bytes 33781760 | tf_op jit(solution)/shard_map/bgrqk,bqgrh->bkgh/dot_general | solution.py:203
  551.2 7.9 copy.60
  559.0 5.9 copy.61
  570.1 14.1 %fusion.74 = bf16[2,1024,5,64]{1,3,2,0:T(8,128)(2,1)} fusion(bf16[2,256,5,3,64]{1,4,3,2,0:T(8,128)(2,1)S(1)} %bitcast.311, f32[2,5,1024,256,3]{3,2,4,1,0:T(8,128)} %get-tuple-element.102, f32[2,5,3,256]{3,2,1,0:T(4,128)S(1)} %copy-done.30), kind=kOutput, calls=%fused_computation.146 | convolution fusion | flops 1023016960 | bytes 33781760 | tf_op jit(solution)/shard_map/bgrqk,bqgrh->bkgh/dot_general | solution.py:203
  585.5 8.3 convolution_multiply_fusion
  593.8 8.8 convolution_multiply_fusion.1
  608.3 35.2 %all-to-all-done.4 = bf16[960,8,4,80]{0,3,1,2:T(8,128)(2,1)} async-done(((bf16[960,8,4,80]{0,3,1,2:T(8,128)(2,1)}), bf16[960,8,4,80]{0,3,1,2:T(8,128)(2,1)}, u32[]{:S(2)}, u32[]{:S(2)}) %all-to-all-start.4) | async-done | bytes 4915232 | tf_op jit(solution)/shard_map/all_to_all | solution.py:253
  663.8 6.1 convolution_bitcast_fusion
  674.4 6.9 fusion.31
  681.3 7.8 copy.54
  689.1 5.7 copy.55
  700.1 12.3 %fusion.41 = f32[960,5120,1]{1,0,2:T(8,128)} fusion(bf16[2,256,2560]{2,1,0:T(8,128)(2,1)} %get-tuple-element.37, bf16[2,256,2560]{2,1,0:T(8,128)(2,1)} %copy-done.95, f32[2,256,960]{1,2,0:T(8,128)} %get-tuple-element.31, f32[960]{0:T(1024)S(1)} %bitcast.342, f32[2,256]{1,0:T(2,128)S(1)} %copy-done.56), kind=kOutput, calls=%fused_computation.84 | convolution fusion | flops 5045125120 | bytes 26875648 | tf_op jit(solution)/shard_map/dot_general | solution.py:60
  712.4 13.8 %fusion.14 = bf16[960,5120]{1,0:T(8,128)(2,1)} fusion(f32[960,5120,1]{1,0,2:T(8,128)} %fusion.41, bf16[2,256,2560]{2,1,0:T(8,128)(2,1)} %get-tuple-element.35, bf16[2,256,2560]{2,1,0:T(8,128)(2,1)} %get-tuple-element.34, f32[2,256,960]{1,2,0:T(8,128)} %get-tuple-element.53, f32[2,256]{1,0:T(2,128)S(1)} %copy-done.60, f32[960]{0:T(1024)S(1)} %bitcast.343), kind=kOutput, calls=%fused_computation.29 | convolution fusion | flops 5054955520 | bytes 36706048 | tf_op jit(solution)/shard_map/dot_general | solution.py:60
  726.1 14.2 %copy.57 = bf16[960,5120]{0,1:T(8,128)(2,1)} copy(bf16[960,5120]{1,0:T(8,128)(2,1)} %fusion.14) | data formatting | bytes 19660800 | tf_op jit(solution)/shard_map/convert_element_type | solution.py:247
  740.4 9.9 copy.58
  750.3 9.2 all-to-all-done
  759.5 6.0 all-to-all-start.2
  770.6 110.4 %all-to-all-done.2 = bf16[960,8,4,160]{0,3,1,2:T(8,128)(2,1)} async-done(((bf16[960,8,4,160]{0,3,1,2:T(8,128)(2,1)}), bf16[960,8,4,160]{0,3,1,2:T(8,128)(2,1)}, u32[]{:S(2)}, u32[]{:S(2)}) %all-to-all-start.2) | async-done | bytes 9830432 | tf_op jit(solution)/shard_map/all_to_all | solution.py:246
  881.0 6.3 all-to-all-start.1
  887.9 9.2 reduce_sum.271
  897.2 21.3 %all-to-all-done.1 = bf16[960,8,80]{0,2,1:T(8,128)(2,1)} async-done(((bf16[960,8,80]{0,2,1:T(8,128)(2,1)}), bf16[960,8,80]{0,2,1:T(8,128)(2,1)}, u32[]{:S(2)}, u32[]{:S(2)}) %all-to-all-start.1) | async-done | bytes 1228832 | tf_op jit(solution)/shard_map/all_to_all | solution.py:263
  930.2 6.3 fusion.52
  938.1 63.9 %all-reduce = (f32[]{:T(128)}, f32[]{:T(128)}, f32[2,960]{1,0:T(2,128)}, f32[960]{0:T(1024)}) all-reduce(f32[]{:T(128)S(6)} %add.239, f32[]{:T(128)} %convert_reduce_fusion.3, f32[2,960]{1,0:T(2,128)S(1)} %pad_maximum_fusion.26, f32[960]{0:T(1024)S(1)} %add.263), channel_id=1, replica_groups=mesh['dp'=8,'ctx'=4] {'dp','ctx'}, use_global_device_ids=true, to_apply=%region_10.11 | all-reduce | flops 2882 | bytes 23056 | tf_op jit(solution)/shard_map/psum | solution.py:275
  (309 shorter events, 142.4 us)
Async XLA Ops:
  7.2 71.7 %copy-start = (bf16[4,256,960]{1,2,0:T(8,128)(2,1)S(1)}, bf16[4,256,960]{1,2,0:T(8,128)(2,1)}, u32[]{:S(2)}) copy-start(bf16[4,256,960]{1,2,0:T(8,128)(2,1)} %param.9) | copy-start | bytes 5898244
  7.2 71.7 %all-gather.8.cloned.1.call-start = ((), (), s32[]{:S(2)}) async-start(), calls=%async_computation.10 | async-start | bytes 5406720 | tf_op jit(solution)/shard_map/all_gather | solution.py:107
  7.9 102.6 %all-gather.20.cloned.1.call-start = ((), (), s32[]{:S(2)}) async-start(), calls=%async_computation.16 | async-start | bytes 1638400 | tf_op jit(solution)/shard_map/all_gather | solution.py:126
  10.5 72.5 %copy-start.75 = (f32[2,256]{1,0:T(2,128)}, f32[2,256]{1,0:T(2,128)S(1)}, u32[]{:S(2)}) copy-start(f32[2,256]{1,0:T(2,128)S(1)} %get-tuple-element.88) | copy-start | bytes 6148
  10.5 72.5 %copy-start.71 = (f32[2,256]{1,0:T(2,128)}, f32[2,256]{1,0:T(2,128)S(1)}, u32[]{:S(2)}) copy-start(f32[2,256]{1,0:T(2,128)S(1)} %get-tuple-element.110) | copy-start | bytes 6148
  10.5 72.5 %copy-start.49 = (f32[1,960]{1,0:T(1,128)}, f32[1,960]{1,0:T(1,128)S(1)}, u32[]{:S(2)}) copy-start(f32[1,960]{1,0:T(1,128)S(1)} %get-tuple-element.71) | copy-start | bytes 11524
  10.5 379.4 %copy-start.44 = (f32[1,960]{1,0:T(1,128)}, f32[1,960]{1,0:T(1,128)S(1)}, u32[]{:S(2)}) copy-start(f32[1,960]{1,0:T(1,128)S(1)} %get-tuple-element.70) | copy-start | bytes 11524
  10.7 96.1 %copy-start.38 = (f32[256,32]{0,1:T(8,128)}, f32[256,32]{0,1:T(8,128)S(1)}, u32[]{:S(2)}) copy-start(f32[256,32]{0,1:T(8,128)S(1)} %get-tuple-element.95) | copy-start | bytes 98308
  10.8 96.1 %copy-start.40 = (f32[256,32]{0,1:T(8,128)}, f32[256,32]{0,1:T(8,128)S(1)}, u32[]{:S(2)}) copy-start(f32[256,32]{0,1:T(8,128)S(1)} %get-tuple-element.96) | copy-start | bytes 98308
  87.7 50.7 %all-gather.12.cloned.1.call-start = ((), (), s32[]{:S(2)}) async-start(), calls=%async_computation.12 | async-start | bytes 1638400 | tf_op jit(solution)/shard_map/all_gather | solution.py:126
  88.5 77.4 %all-gather.18.cloned.1.call-start = ((), (), s32[]{:S(2)}) async-start(), calls=%async_computation.15 | async-start | bytes 1638400 | tf_op jit(solution)/shard_map/all_gather | solution.py:127
  90.5 93.2 %all-gather.10.cloned.1.call-start = ((), (), s32[]{:S(2)}) async-start(), calls=%async_computation.11 | async-start | bytes 1638400 | tf_op jit(solution)/shard_map/all_gather | solution.py:127
  92.4 161.9 %all-gather.14.cloned.1.call-start = ((), (), s32[]{:S(2)}) async-start(), calls=%async_computation.13 | async-start | bytes 10813440 | tf_op jit(solution)/shard_map/all_gather | solution.py:108
  93.0 228.0 %all-gather.16.cloned.1.call-start = ((), (), s32[]{:S(2)}) async-start(), calls=%async_computation.14 | async-start | bytes 5406720 | tf_op jit(solution)/shard_map/all_gather | solution.py:109
  93.7 564.2 %reduce-scatter.9.cloned.1.call-start = ((), (), s32[]{:S(2)}) async-start(), calls=%async_computation.19 | async-start | bytes 1638400 | tf_op jit(solution)/shard_map/reduce_scatter | solution.py:210
  110.5 15.0 %copy-start.21 = (bf16[2,256,15,32]{1,3,2,0:T(8,128)(2,1)}, bf16[2,256,15,32]{1,3,2,0:T(8,128)(2,1)S(1)}, u32[]{:S(2)}) copy-start(bf16[2,256,15,32]{1,3,2,0:T(8,128)(2,1)S(1)} %get-tuple-element.66) | copy-start | bytes 1474564
  110.5 28.0 %copy-start.18 = (bf16[2,256,15,32]{1,3,2,0:T(8,128)(2,1)}, bf16[2,256,15,32]{1,3,2,0:T(8,128)(2,1)S(1)}, u32[]{:S(2)}) copy-start(bf16[2,256,15,32]{1,3,2,0:T(8,128)(2,1)S(1)} %get-tuple-element.48) | copy-start | bytes 1474564
  110.5 28.0 %copy-start.20 = (bf16[2,256,15,32]{1,3,2,0:T(8,128)(2,1)}, bf16[2,256,15,32]{1,3,2,0:T(8,128)(2,1)S(1)}, u32[]{:S(2)}) copy-start(bf16[2,256,15,32]{1,3,2,0:T(8,128)(2,1)S(1)} %get-tuple-element.49) | copy-start | bytes 1474564
  203.0 187.0 %copy-start.53 = (f32[2,256]{1,0:T(2,128)}, f32[2,256]{1,0:T(2,128)S(1)}, u32[]{:S(2)}) copy-start(f32[2,256]{1,0:T(2,128)S(1)} %get-tuple-element.91) | copy-start | bytes 6148
  203.0 187.0 %copy-start.55 = (f32[2,256]{1,0:T(2,128)}, f32[2,256]{1,0:T(2,128)S(1)}, u32[]{:S(2)}) copy-start(f32[2,256]{1,0:T(2,128)S(1)} %get-tuple-element.92) | copy-start | bytes 6148
  203.0 187.0 %copy-start.57 = (f32[2,256]{1,0:T(2,128)}, f32[2,256]{1,0:T(2,128)S(1)}, u32[]{:S(2)}) copy-start(f32[2,256]{1,0:T(2,128)S(1)} %get-tuple-element.89) | copy-start | bytes 6148
  203.0 187.0 %copy-start.59 = (f32[2,256]{1,0:T(2,128)}, f32[2,256]{1,0:T(2,128)S(1)}, u32[]{:S(2)}) copy-start(f32[2,256]{1,0:T(2,128)S(1)} %get-tuple-element.90) | copy-start | bytes 6148
  329.1 21.8 %slice-start = ((s8[10485760]{0:T(1024)(128)(4,1)}), s8[4194304]{0:T(1024)(128)(4,1)S(1)}, s32[]{:S(2)}) async-start(s8[10485760]{0:T(1024)(128)(4,1)} %bitcast.308), calls=%async_computation.21 | async-start | bytes 8388608
  329.1 21.8 %slice-start.1 = ((s8[10485760]{0:T(1024)(128)(4,1)}), s8[4194304]{0:T(1024)(128)(4,1)S(1)}, s32[]{:S(2)}) async-start(s8[10485760]{0:T(1024)(128)(4,1)} %bitcast.308), calls=%async_computation.22 | async-start | bytes 8388608
  375.0 15.0 %copy-start.3 = (f32[2,256,960]{1,2,0:T(8,128)S(1)}, f32[2,256,960]{1,2,0:T(8,128)}, u32[]{:S(2)}) copy-start(f32[2,256,960]{1,2,0:T(8,128)} %copy-done.2) | copy-start | bytes 5898244
  399.1 24.2 %copy-start.9 = (bf16[2,256,960]{1,2,0:T(8,128)(2,1)}, bf16[2,256,960]{1,2,0:T(8,128)(2,1)S(1)}, u32[]{:S(2)}) copy-start(bf16[2,256,960]{1,2,0:T(8,128)(2,1)S(1)} %convolution_convert_fusion) | copy-start | bytes 2949124
  423.3 26.8 %copy-start.22 = (bf16[2,256,15,32]{1,3,2,0:T(8,128)(2,1)S(1)}, bf16[2,256,15,32]{1,3,2,0:T(8,128)(2,1)}, u32[]{:S(2)}) copy-start(bf16[2,256,15,32]{1,3,2,0:T(8,128)(2,1)} %copy-done.21) | copy-start | bytes 1474564
  423.3 26.8 %copy-start.23 = (bf16[2,256,15,32]{1,3,2,0:T(8,128)(2,1)S(1)}, bf16[2,256,15,32]{1,3,2,0:T(8,128)(2,1)}, u32[]{:S(2)}) copy-start(bf16[2,256,15,32]{1,3,2,0:T(8,128)(2,1)} %get-tuple-element.67) | copy-start | bytes 1474564
  461.5 198.3 %reduce-scatter.5.cloned.1.call-start = ((), (), s32[]{:S(2)}) async-start(), calls=%async_computation.17 | async-start | bytes 1638400 | tf_op jit(solution)/shard_map/reduce_scatter | solution.py:210
  489.1 26.6 %copy-start.19 = (bf16[2,256,15,32]{1,3,2,0:T(8,128)(2,1)S(1)}, bf16[2,256,15,32]{1,3,2,0:T(8,128)(2,1)}, u32[]{:S(2)}) copy-start(bf16[2,256,15,32]{1,3,2,0:T(8,128)(2,1)} %copy-done.18) | copy-start | bytes 1474564
  527.3 136.5 %reduce-scatter.11.cloned.1.call-start = ((), (), s32[]{:S(2)}) async-start(), calls=%async_computation.20 | async-start | bytes 1638400 | tf_op jit(solution)/shard_map/reduce_scatter | solution.py:213
  564.9 78.5 %all-to-all-start.4 = ((bf16[960,8,4,80]{0,3,1,2:T(8,128)(2,1)}), bf16[960,8,4,80]{0,3,1,2:T(8,128)(2,1)}, u32[]{:S(2)}, u32[]{:S(2)}) async-start(bf16[960,8,4,80]{0,3,1,2:T(8,128)(2,1)} %copy.61), calls=%async_computation.8 | async-start | bytes 10485760 | tf_op jit(solution)/shard_map/all_to_all | solution.py:253
  570.0 99.9 %reduce-scatter.7.cloned.1.call-start = ((), (), s32[]{:S(2)}) async-start(), calls=%async_computation.18 | async-start | bytes 1638400 | tf_op jit(solution)/shard_map/reduce_scatter | solution.py:213
  648.7 46.1 %all-to-all-start.5 = ((bf16[960,8,80]{0,2,1:T(8,128)(2,1)}), bf16[960,8,80]{0,2,1:T(8,128)(2,1)S(1)}, u32[]{:S(2)}, u32[]{:S(2)}) async-start(bf16[960,8,80]{0,2,1:T(8,128)(2,1)} %reduce_sum.273), calls=%async_computation.9 | async-start | bytes 2621440 | tf_op jit(solution)/shard_map/all_to_all | solution.py:269
  694.8 64.7 %all-to-all-start = ((bf16[960,8,4,80]{0,3,1,2:T(8,128)(2,1)}), bf16[960,8,4,80]{0,3,1,2:T(8,128)(2,1)}, u32[]{:S(2)}, u32[]{:S(2)}) async-start(bf16[960,8,4,80]{0,3,1,2:T(8,128)(2,1)} %copy.55), calls=%async_computation.4 | async-start | bytes 10485760 | tf_op jit(solution)/shard_map/all_to_all | solution.py:239
  759.5 121.6 %all-to-all-start.2 = ((bf16[960,8,4,160]{0,3,1,2:T(8,128)(2,1)}), bf16[960,8,4,160]{0,3,1,2:T(8,128)(2,1)}, u32[]{:S(2)}, u32[]{:S(2)}) async-start(bf16[960,8,4,160]{0,3,1,2:T(8,128)(2,1)} %copy.58), calls=%async_computation.6 | async-start | bytes 20971520 | tf_op jit(solution)/shard_map/all_to_all | solution.py:246
  770.6 116.7 %copy-start.70 = (s32[4,256]{1,0:T(4,128)S(1)}, s32[4,256]{1,0:T(4,128)}, u32[]{:S(2)}) copy-start(s32[4,256]{1,0:T(4,128)} %param.11) | copy-start | bytes 12292
  881.0 37.4 %all-to-all-start.1 = ((bf16[960,8,80]{0,2,1:T(8,128)(2,1)}), bf16[960,8,80]{0,2,1:T(8,128)(2,1)}, u32[]{:S(2)}, u32[]{:S(2)}) async-start(bf16[960,8,80]{0,2,1:T(8,128)(2,1)} %reduce_sum.269), calls=%async_computation.5 | async-start | bytes 2621440 | tf_op jit(solution)/shard_map/all_to_all | solution.py:263
  897.2 25.7 %copy-start.52 = (f32[4,256]{1,0:T(4,128)S(1)}, f32[4,256]{1,0:T(4,128)}, u32[]{:S(2)}) copy-start(f32[4,256]{1,0:T(4,128)} %copy-done.51) | copy-start | bytes 12292
  897.2 25.7 %copy-start.66 = (f32[1,2,256]{2,0,1:T(1,128)S(1)}, f32[1,2,256]{2,0,1:T(1,128)}, u32[]{:S(2)}) copy-start(f32[1,2,256]{2,0,1:T(1,128)} %copy-done.65) | copy-start | bytes 6148
  897.2 25.7 %copy-start.68 = (f32[1,2,256]{2,0,1:T(1,128)S(1)}, f32[1,2,256]{2,0,1:T(1,128)}, u32[]{:S(2)}) copy-start(f32[1,2,256]{2,0,1:T(1,128)} %copy-done.67) | copy-start | bytes 6148
  897.2 25.8 %copy-start.84 = (f32[2,256]{1,0:T(2,128)S(1)}, f32[2,256]{1,0:T(2,128)}, u32[]{:S(2)}) copy-start(f32[2,256]{1,0:T(2,128)} %get-tuple-element.20) | copy-start | bytes 6148
  897.2 25.8 %copy-start.85 = (f32[2,256]{1,0:T(2,128)S(1)}, f32[2,256]{1,0:T(2,128)}, u32[]{:S(2)}) copy-start(f32[2,256]{1,0:T(2,128)} %get-tuple-element.42) | copy-start | bytes 6148
  918.4 97.5 %all-to-all-start.3 = ((bf16[960,8,160]{0,2,1:T(8,128)(2,1)}), bf16[960,8,160]{0,2,1:T(8,128)(2,1)}, u32[]{:S(2)}, u32[]{:S(2)}) async-start(bf16[960,8,160]{0,2,1:T(8,128)(2,1)} %reduce_sum.271), calls=%async_computation.7 | async-start | bytes 5242880 | tf_op jit(solution)/shard_map/all_to_all | solution.py:266
  936.6 66.7 %copy-start.47 = (f32[960]{0:T(1024)S(1)}, f32[960]{0:T(1024)}, u32[]{:S(2)}) copy-start(f32[960]{0:T(1024)} %param.17) | copy-start | bytes 11524
  936.6 66.7 %copy-start.58 = (f32[2,256]{1,0:T(2,128)S(1)}, f32[2,256]{1,0:T(2,128)}, u32[]{:S(2)}) copy-start(f32[2,256]{1,0:T(2,128)} %copy-done.57) | copy-start | bytes 6148
  936.6 66.7 %copy-start.64 = (f32[2,256]{1,0:T(2,128)S(1)}, f32[2,256]{1,0:T(2,128)}, u32[]{:S(2)}) copy-start(f32[2,256]{1,0:T(2,128)} %copy-done.63) | copy-start | bytes 6148
  936.6 66.7 %copy-start.74 = (f32[2,256]{1,0:T(2,128)S(1)}, f32[2,256]{1,0:T(2,128)}, u32[]{:S(2)}) copy-start(f32[2,256]{1,0:T(2,128)} %get-tuple-element.87) | copy-start | bytes 6148
  (70 other events, 384.9 us)
Sparse Core Ops, SparseCore 0:
  10.8 68.0 all-gather.7
  87.8 16.8 all-gather.19
  106.9 18.3 all-gather.11
  127.2 18.3 all-gather.17
  146.9 18.3 all-gather.9
  168.0 86.2 all-gather.13
  257.1 63.8 all-gather.15
  461.7 24.9 reduce-scatter.8
  527.4 24.9 reduce-scatter.4
  555.3 33.5 reduce-scatter.10
  591.5 33.5 reduce-scatter.6
where the time goes:
time: 1030 us
  matrix products  347 us (34%)
  waiting for transfers between devices  333 us (32%)
  other arithmetic  149 us (14%)
  blocking collectives  74.7 us (7%)
  local copies, waits for them, and re-layouts  71.1 us (7%)
  starting transfers between devices  31.9 us (3%)
  between operations  19.2 us (2%)
    all_to_all x1, waiting for transfers between devices, on_device(): lax.all_to_all(owner_layout(grad_gu).astype(jnp.bfloat16), 'ctx', split_a...  110 us
    all_gather x1, waiting for transfers between devices, on_device(): lax.all_gather(packs[0], ('dp', 'ctx'), axis=1, tiled=True)  68.1 us
    dot_general x8, matrix products, by_columns(): lax.dot_general(left, right, (((2,), (1,)), ((), ())), preferred_element_...  67.6 us
    psum x1, blocking collectives, on_device(): lax.psum((energy, grad_gains, grad_router), ('dp', 'ctx'))  63.9 us
    convert_element_type x2, other arithmetic, on_device(): (probs * (d_probs - jnp.sum(probs * d_probs, axis=-1, keepdims=True))).as...  53.3 us
    dot_general x8, matrix products, over_rows(): lax.dot_general(left, right, (((0, 1), (0, 1)), ((), ())), preferred_elem...  51 us
    all_gather x1, waiting for transfers between devices, on_device(): lax.all_gather(packs[1], ('dp', 'ctx'), axis=1, tiled=True)  50.6 us
    dot_general x2, matrix products, on_device(): jnp.einsum('bqgrh,bkgh->bgrqk', d_heads_low, values_all, preferred_elemen...  48.6 us
  transfers between devices with their start and end apart: 17, of which 7 were waited for; matrix products, arithmetic and copies ran while one was open for 39% of the time, Pallas kernels for 0%

commit v1 on v0

--- a/solution.py
+++ b/solution.py
@@ -69,6 +69,16 @@
 
 
 def on_device(states, teacher, validity, chosen, attn_pack, gate_up, down_proj, norm_gains, router):
+
+    def create_run_now(m):
+        big = lax.all_to_all(
+            jnp.stack(jnp.split(m, lax.axis_size("dp"), axis=1), axis=0),
+            axis_name="dp",
+            split_axis=0,
+            concat_axis=0,
+        )
+        return jnp.concatenate(big, axis=1)
+
     seq_count, block_rows, width = states.shape
     seq_micro = seq_count // MICRO
     ctx_count = lax.axis_size("ctx")
@@ -260,9 +270,7 @@
     )
     attn_ctx, gu_ctx, down_ctx = [jnp.sum(piece, axis=2) for piece in by_ctx]
     by_dp = (
-        lax.all_to_all(shortened(attn_ctx), "dp", split_axis=1, concat_axis=1, tiled=True).astype(
-            attn_ctx.dtype
-        ),
+        create_run_now(shortened(attn_ctx)).astype(attn_ctx.dtype),
         lax.all_to_all(shortened(gu_ctx), "dp", split_axis=1, concat_axis=1, tiled=True).astype(
             gu_ctx.dtype
         ),

time: 1030 us -> 1030 us (level)
  local copies, waits for them, and re-layouts: 71.1 us -> 83.9 us
  waiting for transfers between devices: 333 us -> 321 us
    all_to_all x1, waiting for transfers between devices: 110 us -> 97.7 us  [on_device(): lax.all_to_all(owner_layout(grad_gu).astype(jnp.bfloat16), 'ctx', split_a...]
    unnamed x198 -> x205, local copies, waits for them, and re-layouts: 13.2 us -> 24.4 us
  transfers between devices with their start and end apart: 17 -> 17, of which waited for: 7 -> 7; matrix products, arithmetic and copies ran while one was open for 39% -> 40% of each run, Pallas kernels for 0% -> 0%
where the time goes in v1:
time: 1030 us
  matrix products  347 us (34%)
  waiting for transfers between devices  321 us (31%)
  other arithmetic  149 us (14%)
  local copies, waits for them, and re-layouts  83.9 us (8%)
  blocking collectives  74.7 us (7%)
  starting transfers between devices  31.9 us (3%)
  between operations  19.2 us (2%)
    all_to_all x1, waiting for transfers between devices, on_device(): lax.all_to_all(owner_layout(grad_gu).astype(jnp.bfloat16), 'ctx', split_a...  97.7 us
    all_gather x1, waiting for transfers between devices, on_device(): lax.all_gather(packs[0], ('dp', 'ctx'), axis=1, tiled=True)  68.1 us
    dot_general x8, matrix products, by_columns(): lax.dot_general(left, right, (((2,), (1,)), ((), ())), preferred_element_...  67.6 us
    psum x1, blocking collectives, on_device(): lax.psum((energy, grad_gains, grad_router), ('dp', 'ctx'))  63.9 us
    convert_element_type x2, other arithmetic, on_device(): (probs * (d_probs - jnp.sum(probs * d_probs, axis=-1, keepdims=True))).as...  53.3 us
    dot_general x8, matrix products, over_rows(): lax.dot_general(left, right, (((0, 1), (0, 1)), ((), ())), preferred_elem...  51 us
    all_gather x1, waiting for transfers between devices, on_device(): lax.all_gather(packs[1], ('dp', 'ctx'), axis=1, tiled=True)  50.6 us
    dot_general x2, matrix products, on_device(): jnp.einsum('bqgrh,bkgh->bgrqk', d_heads_low, values_all, preferred_elemen...  48.6 us
  transfers between devices with their start and end apart: 17, of which 7 were waited for; matrix products, arithmetic and copies ran while one was open for 40% of the time, Pallas kernels for 0%

profile of v1, /device:TPU:0, one launch (start us, length us, event | category | flops | bytes accessed | tf_op | source)
XLA Modules:
  0.0 1026.9 jit_solution(2927333009687302043)
XLA Ops:
  10.8 68.1 %all-gather.8.cloned.1.call-done = bf16[960,2560]{0,1:T(8,128)(2,1)} async-done(((bf16[960,80]{0,1:T(8,128)(2,1)}), bf16[960,2560]{0,1:T(8,128)(2,1)}) %all-gather.8.cloned.1.call-update) | async-done | bytes 4915216 | tf_op jit(solution)/shard_map/all_gather | solution.py:117
  110.5 15.0 %bitcast_reduce_fusion = (f32[2,5,3,256]{3,2,1,0:T(4,128)S(1)}, f32[2,5,1024,256,3]{3,2,4,1,0:T(8,128)}) fusion(bf16[2,256,5,3,32]{1,4,3,2,0:T(8,128)(2,1)S(1)} %bitcast.354, bf16[2,256,5,3,32]{1,4,3,2,0:T(8,128)(2,1)} %bitcast.356, bf16[2,1024,5,64]{1,3,2,0:T(8,128)(2,1)} %all-gather.20.cloned.1.call-done, pred[2,1024]{1,0:T(4,128)(4,1)S(1)} %get-tuple-element.98), kind=kOutput, calls=%fused_computation.12 | convolution fusion | flops 1032184320 | bytes 33783808 | tf_op jit(solution)/shard_map/bqgrh,bkgh->bgrqk/dot_general | solution.py:54
  125.5 13.0 %fusion.11 = f32[2,5,3,256]{3,2,1,0:T(4,128)S(1)} fusion(f32[2,5,1024,256,3]{3,2,4,1,0:T(8,128)} %get-tuple-element.100, f32[2,5,3,256]{3,2,1,0:T(4,128)S(1)} %get-tuple-element.99), kind=kLoop, calls=%fused_computation.25 | loop fusion | flops 15720960 | bytes 31518720 | tf_op jit(solution)/shard_map/reduce_sum | solution.py:144
  138.5 14.3 %bitcast_reduce_fusion.1 = (f32[2,5,3,256]{3,2,1,0:T(4,128)S(1)}, f32[2,5,1024,256,3]{3,2,4,1,0:T(8,128)}) fusion(bf16[2,256,5,3,32]{1,4,3,2,0:T(8,128)(2,1)S(1)} %bitcast.352, bf16[2,256,5,3,32]{1,4,3,2,0:T(8,128)(2,1)S(1)} %bitcast.350, bf16[2,1024,5,64]{1,3,2,0:T(8,128)(2,1)} %all-gather.12.cloned.1.call-done, pred[2,1024]{1,0:T(4,128)(4,1)S(1)} %get-tuple-element.97), kind=kOutput, calls=%fused_computation.17 | convolution fusion | flops 1032184320 | bytes 33783808 | tf_op jit(solution)/shard_map/bqgrh,bkgh->bgrqk/dot_general | solution.py:54
  152.8 13.1 %fusion.10 = f32[2,5,3,256]{3,2,1,0:T(4,128)S(1)} fusion(f32[2,5,1024,256,3]{3,2,4,1,0:T(8,128)} %get-tuple-element.102, f32[2,5,3,256]{3,2,1,0:T(4,128)S(1)} %get-tuple-element.101), kind=kLoop, calls=%fused_computation.24 | loop fusion | flops 15720960 | bytes 31518720 | tf_op jit(solution)/shard_map/reduce_sum | solution.py:144
  166.0 13.3 %fusion.72 = bf16[2,5,64,3,256]{4,2,3,1,0:T(8,128)(2,1)S(1)} fusion(f32[2,5,1024,256,3]{3,2,4,1,0:T(8,128)} %get-tuple-element.100, f32[2,5,3,256]{3,2,1,0:T(4,128)S(1)} %fusion.11, f32[2,5,3,256]{3,2,1,0:T(4,128)S(1)} %get-tuple-element.99, bf16[2,1024,5,64]{1,3,2,0:T(8,128)(2,1)} %all-gather.18.cloned.1.call-done), kind=kOutput, calls=%fused_computation.144 | convolution fusion | flops 1030717440 | bytes 33812480 | tf_op jit(solution)/shard_map/bgrqk,bkgh->bqgrh/dot_general | solution.py:147
  183.7 13.5 %fusion.73 = bf16[2,5,64,3,256]{4,2,3,1,0:T(8,128)(2,1)S(1)} fusion(f32[2,5,1024,256,3]{3,2,4,1,0:T(8,128)} %get-tuple-element.102, f32[2,5,3,256]{3,2,1,0:T(4,128)S(1)} %fusion.10, f32[2,5,3,256]{3,2,1,0:T(4,128)S(1)} %get-tuple-element.101, bf16[2,1024,5,64]{1,3,2,0:T(8,128)(2,1)} %all-gather.10.cloned.1.call-done), kind=kOutput, calls=%fused_computation.145 | convolution fusion | flops 1030717440 | bytes 33812480 | tf_op jit(solution)/shard_map/bgrqk,bkgh->bqgrh/dot_general | solution.py:147
  197.2 5.7 multiply_reduce_fusion.9
  203.7 50.6 %all-gather.14.cloned.1.call-done = bf16[960,5120]{0,1:T(8,128)(2,1)} async-done(((bf16[960,160]{0,1:T(8,128)(2,1)}), bf16[960,5120]{0,1:T(8,128)(2,1)}) %all-gather.14.cloned.1.call-update) | async-done | bytes 9830416 | tf_op jit(solution)/shard_map/all_gather | solution.py:118
  254.3 9.5 fusion.27
  268.8 8.9 fusion.29
  284.5 36.5 %all-gather.16.cloned.1.call-done = bf16[960,2560]{0,1:T(8,128)(2,1)} async-done(((bf16[960,80]{0,1:T(8,128)(2,1)}), bf16[960,2560]{0,1:T(8,128)(2,1)}) %all-gather.16.cloned.1.call-update) | async-done | bytes 4915216 | tf_op jit(solution)/shard_map/all_gather | solution.py:119
  321.0 8.0 fusion.66
  329.1 10.3 multiply_reduce_fusion.3
  339.4 11.5 %multiply_convert_fusion.3 = (bf16[2,256,2560]{2,1,0:T(8,128)(2,1)S(1)}, bf16[2,256,2560]{2,1,0:T(8,128)(2,1)}) fusion(f32[2,256,5120]{2,1,0:T(8,128)} %copy-done.6, bf16[960,2560]{0,1:T(8,128)(2,1)} %all-gather.16.cloned.1.call-done, f32[2,256,960]{1,2,0:T(8,128)S(1)} %get-tuple-element.43, f32[2,256]{1,0:T(2,128)S(1)} %copy-done.48), kind=kOutput, calls=%fused_computation.62 | convolution fusion | flops 2534604800 | bytes 22611968 | tf_op jit(solution)/shard_map/dot_general | solution.py:180
  350.9 10.2 multiply_convert_fusion.1
  361.1 13.9 %fusion.25 = f32[2,256,960]{1,2,0:T(8,128)} fusion(bf16[960,5120]{0,1:T(8,128)(2,1)} %all-gather.14.cloned.1.call-done, bf16[2,256,2560]{2,1,0:T(8,128)(2,1)} %get-tuple-element.37, bf16[2,256,2560]{2,1,0:T(8,128)(2,1)S(1)} %get-tuple-element.36), kind=kOutput, calls=%fused_computation.38 | convolution fusion | flops 5043650560 | bytes 17039360 | tf_op jit(solution)/shard_map/dot_general | solution.py:66
  375.0 15.0 %multiply_reduce_fusion = (f32[960]{0:T(1024)}, f32[2,256]{1,0:T(2,128)S(1)}, f32[2,256]{1,0:T(2,128)S(1)}, f32[960]{0:T(1024)}, f32[2,256,960]{1,2,0:T(8,128)}) fusion(f32[2,256,960]{1,2,0:T(8,128)} %get-tuple-element.53, f32[2,256]{1,0:T(2,128)S(1)} %get-tuple-element.90, f32[960]{0:T(1024)S(1)} %bitcast.372, f32[2,256,960]{1,2,0:T(8,128)} %get-tuple-element.31, ...), kind=kOutput, calls=%fused_computation.116 | convolution fusion | flops 5049545728 | bytes 22957312 | tf_op jit(solution)/shard_map/dot_general | solution.py:66
  390.0 5.9 add_convert_fusion
  399.2 24.1 %fusion = (f32[2,5,3,256]{3,2,1,0:T(4,128)S(1)}, f32[2,5,1024,256,3]{3,2,4,1,0:T(8,128)}) fusion(f32[2,5,1024,256,3]{3,2,4,1,0:T(8,128)} %get-tuple-element.100, f32[2,5,3,256]{3,2,1,0:T(4,128)S(1)} %log_add_fusion, bf16[2,256,5,3,64]{1,4,3,2,0:T(8,128)(2,1)S(1)} %bitcast.344, bf16[2,1024,5,64]{1,3,2,0:T(8,128)(2,1)S(1)} %copy-done.26), kind=kOutput, calls=%fused_computation.2 | convolution fusion | flops 1030218240 | bytes 65269760 | tf_op jit(solution)/shard_map/bqgrh,bkgh->bgrqk/dot_general | solution.py:197
  423.3 26.8 %fusion.2 = bf16[2,5,3,256,1024]{3,4,2,1,0:T(8,128)(2,1)} fusion(f32[2,5,1024,256,3]{3,2,4,1,0:T(8,128)} %get-tuple-element.106, f32[2,5,1024,256,3]{3,2,4,1,0:T(8,128)} %get-tuple-element.100, f32[2,5,3,256]{3,2,1,0:T(4,128)S(1)} %get-tuple-element.105, f32[2,5,3,256]{3,2,1,0:T(4,128)S(1)} %log_add_fusion), kind=kLoop, calls=%fused_computation.4 | loop fusion | flops 31457280 | bytes 78704640 | tf_op jit(solution)/shard_map/convert_element_type | solution.py:200
  450.1 11.4 %fusion.81 = bf16[2,1024,5,64]{1,3,2,0:T(8,128)(2,1)} fusion(bf16[2,5,3,256,1024]{3,4,2,1,0:T(8,128)(2,1)} %fusion.2, bf16[2,256,5,3,32]{1,4,3,2,0:T(8,128)(2,1)S(1)} %bitcast.355, bf16[2,256,5,3,32]{1,4,3,2,0:T(8,128)(2,1)S(1)} %bitcast.357), kind=kOutput, calls=%fused_computation.149 | convolution fusion | flops 1009909760 | bytes 18022400 | tf_op jit(solution)/shard_map/bgrqk,bqgrh->bkgh/dot_general | solution.py:208
  464.7 24.4 %fusion.3 = (f32[2,5,3,256]{3,2,1,0:T(4,128)S(1)}, f32[2,5,1024,256,3]{3,2,4,1,0:T(8,128)}) fusion(f32[2,5,1024,256,3]{3,2,4,1,0:T(8,128)} %get-tuple-element.102, f32[2,5,3,256]{3,2,1,0:T(4,128)S(1)} %copy-done.30, bf16[2,256,5,3,64]{1,4,3,2,0:T(8,128)(2,1)S(1)} %bitcast.342, bf16[2,1024,5,64]{1,3,2,0:T(8,128)(2,1)S(1)} %copy-done.25), kind=kOutput, calls=%fused_computation.7 | convolution fusion | flops 1030218240 | bytes 65269760 | tf_op jit(solution)/shard_map/bqgrh,bkgh->bgrqk/dot_general | solution.py:197
  489.1 26.6 %fusion.5 = bf16[2,5,3,256,1024]{3,4,2,1,0:T(8,128)(2,1)} fusion(f32[2,5,1024,256,3]{3,2,4,1,0:T(8,128)} %get-tuple-element.108, f32[2,5,1024,256,3]{3,2,4,1,0:T(8,128)} %get-tuple-element.102, f32[2,5,3,256]{3,2,1,0:T(4,128)S(1)} %get-tuple-element.107, f32[2,5,3,256]{3,2,1,0:T(4,128)S(1)} %copy-done.30), kind=kLoop, calls=%fused_computation.9 | loop fusion | flops 31457280 | bytes 78704640 | tf_op jit(solution)/shard_map/convert_element_type | solution.py:200
  515.7 11.5 %fusion.80 = bf16[2,1024,5,64]{1,3,2,0:T(8,128)(2,1)} fusion(bf16[2,5,3,256,1024]{3,4,2,1,0:T(8,128)(2,1)} %fusion.5, bf16[2,256,5,3,32]{1,4,3,2,0:T(8,128)(2,1)} %bitcast.353, bf16[2,256,5,3,32]{1,4,3,2,0:T(8,128)(2,1)S(1)} %bitcast.351), kind=kOutput, calls=%fused_computation.148 | convolution fusion | flops 1009909760 | bytes 18022400 | tf_op jit(solution)/shard_map/bgrqk,bqgrh->bkgh/dot_general | solution.py:208
  527.3 14.8 %fusion.77 = bf16[2,1024,5,64]{1,3,2,0:T(8,128)(2,1)} fusion(bf16[2,256,5,3,64]{1,4,3,2,0:T(8,128)(2,1)} %bitcast.345, f32[2,5,1024,256,3]{3,2,4,1,0:T(8,128)} %get-tuple-element.100, f32[2,5,3,256]{3,2,1,0:T(4,128)S(1)} %log_add_fusion), kind=kOutput, calls=%fused_computation.147 | convolution fusion | flops 1023016960 | bytes 33781760 | tf_op jit(solution)/shard_map/bgrqk,bqgrh->bkgh/dot_general | solution.py:213
  551.2 7.9 copy.66
  559.0 5.9 copy.67
  570.1 14.1 %fusion.74 = bf16[2,1024,5,64]{1,3,2,0:T(8,128)(2,1)} fusion(bf16[2,256,5,3,64]{1,4,3,2,0:T(8,128)(2,1)S(1)} %bitcast.343, f32[2,5,1024,256,3]{3,2,4,1,0:T(8,128)} %get-tuple-element.102, f32[2,5,3,256]{3,2,1,0:T(4,128)S(1)} %copy-done.30), kind=kOutput, calls=%fused_computation.146 | convolution fusion | flops 1023016960 | bytes 33781760 | tf_op jit(solution)/shard_map/bgrqk,bqgrh->bkgh/dot_general | solution.py:213
  585.5 8.3 convolution_multiply_fusion
  593.8 8.8 convolution_multiply_fusion.1
  608.3 35.2 %all-to-all-done.4 = bf16[960,8,4,80]{0,3,1,2:T(8,128)(2,1)} async-done(((bf16[960,8,4,80]{0,3,1,2:T(8,128)(2,1)}), bf16[960,8,4,80]{0,3,1,2:T(8,128)(2,1)}, u32[]{:S(2)}, u32[]{:S(2)}) %all-to-all-start.4) | async-done | bytes 4915232 | tf_op jit(solution)/shard_map/all_to_all | solution.py:263
  663.8 6.1 convolution_bitcast_fusion
  674.4 6.9 fusion.31
  681.3 7.8 copy.61
  689.1 5.7 copy.62
  700.1 12.3 %fusion.41 = f32[960,5120,1]{1,0,2:T(8,128)} fusion(bf16[2,256,2560]{2,1,0:T(8,128)(2,1)} %get-tuple-element.37, bf16[2,256,2560]{2,1,0:T(8,128)(2,1)} %copy-done.95, f32[2,256,960]{1,2,0:T(8,128)} %get-tuple-element.31, f32[960]{0:T(1024)S(1)} %bitcast.374, f32[2,256]{1,0:T(2,128)S(1)} %copy-done.56), kind=kOutput, calls=%fused_computation.84 | convolution fusion | flops 5045125120 | bytes 26875648 | tf_op jit(solution)/shard_map/dot_general | solution.py:60
  712.4 13.8 %fusion.14 = bf16[960,5120]{1,0:T(8,128)(2,1)} fusion(f32[960,5120,1]{1,0,2:T(8,128)} %fusion.41, bf16[2,256,2560]{2,1,0:T(8,128)(2,1)} %get-tuple-element.35, bf16[2,256,2560]{2,1,0:T(8,128)(2,1)} %get-tuple-element.34, f32[2,256,960]{1,2,0:T(8,128)} %get-tuple-element.53, f32[2,256]{1,0:T(2,128)S(1)} %copy-done.60, f32[960]{0:T(1024)S(1)} %bitcast.375), kind=kOutput, calls=%fused_computation.29 | convolution fusion | flops 5054955520 | bytes 36706048 | tf_op jit(solution)/shard_map/dot_general | solution.py:60
  726.1 14.2 %copy.63 = bf16[960,5120]{0,1:T(8,128)(2,1)} copy(bf16[960,5120]{1,0:T(8,128)(2,1)} %fusion.14) | data formatting | bytes 19660800 | tf_op jit(solution)/shard_map/convert_element_type | solution.py:257
  740.4 9.9 copy.64
  750.3 9.2 all-to-all-done
  759.5 6.0 all-to-all-start.2
  783.4 97.7 %all-to-all-done.2 = bf16[960,8,4,160]{0,3,1,2:T(8,128)(2,1)} async-done(((bf16[960,8,4,160]{0,3,1,2:T(8,128)(2,1)}), bf16[960,8,4,160]{0,3,1,2:T(8,128)(2,1)}, u32[]{:S(2)}, u32[]{:S(2)}) %all-to-all-start.2) | async-done | bytes 9830432 | tf_op jit(solution)/shard_map/all_to_all | solution.py:256
  881.0 6.3 all-to-all-start.1
  887.9 9.2 reduce_sum.271
  897.2 21.3 %all-to-all-done.1 = bf16[8,960,1,80]{1,3,2,0:T(8,128)(2,1)} async-done(((bf16[8,960,1,80]{1,3,2,0:T(8,128)(2,1)}), bf16[8,960,1,80]{1,3,2,0:T(8,128)(2,1)}, u32[]{:S(2)}, u32[]{:S(2)}) %all-to-all-start.1) | async-done | bytes 1228832 | tf_op jit(solution)/shard_map/all_to_all | solution.py:74
  930.2 6.3 fusion.52
  938.1 63.9 %all-reduce = (f32[]{:T(128)}, f32[]{:T(128)}, f32[2,960]{1,0:T(2,128)}, f32[960]{0:T(1024)}) all-reduce(f32[]{:T(128)S(6)} %add.239, f32[]{:T(128)} %convert_reduce_fusion.3, f32[2,960]{1,0:T(2,128)S(1)} %pad_maximum_fusion.26, f32[960]{0:T(1024)S(1)} %add.263), channel_id=1, replica_groups=mesh['dp'=8,'ctx'=4] {'dp','ctx'}, use_global_device_ids=true, to_apply=%region_10.11 | all-reduce | flops 2882 | bytes 23056 | tf_op jit(solution)/shard_map/psum | solution.py:283
  (317 shorter events, 155.1 us)
Async XLA Ops:
  7.2 71.7 %copy-start = (bf16[4,256,960]{1,2,0:T(8,128)(2,1)S(1)}, bf16[4,256,960]{1,2,0:T(8,128)(2,1)}, u32[]{:S(2)}) copy-start(bf16[4,256,960]{1,2,0:T(8,128)(2,1)} %param.9) | copy-start | bytes 5898244
  7.2 71.7 %all-gather.8.cloned.1.call-start = ((), (), s32[]{:S(2)}) async-start(), calls=%async_computation.10 | async-start | bytes 5406720 | tf_op jit(solution)/shard_map/all_gather | solution.py:117
  7.9 102.6 %all-gather.20.cloned.1.call-start = ((), (), s32[]{:S(2)}) async-start(), calls=%async_computation.16 | async-start | bytes 1638400 | tf_op jit(solution)/shard_map/all_gather | solution.py:136
  10.5 72.5 %copy-start.75 = (f32[2,256]{1,0:T(2,128)}, f32[2,256]{1,0:T(2,128)S(1)}, u32[]{:S(2)}) copy-start(f32[2,256]{1,0:T(2,128)S(1)} %get-tuple-element.88) | copy-start | bytes 6148
  10.5 72.5 %copy-start.71 = (f32[2,256]{1,0:T(2,128)}, f32[2,256]{1,0:T(2,128)S(1)}, u32[]{:S(2)}) copy-start(f32[2,256]{1,0:T(2,128)S(1)} %get-tuple-element.110) | copy-start | bytes 6148
  10.5 72.5 %copy-start.49 = (f32[1,960]{1,0:T(1,128)}, f32[1,960]{1,0:T(1,128)S(1)}, u32[]{:S(2)}) copy-start(f32[1,960]{1,0:T(1,128)S(1)} %get-tuple-element.71) | copy-start | bytes 11524
  10.5 379.4 %copy-start.44 = (f32[1,960]{1,0:T(1,128)}, f32[1,960]{1,0:T(1,128)S(1)}, u32[]{:S(2)}) copy-start(f32[1,960]{1,0:T(1,128)S(1)} %get-tuple-element.70) | copy-start | bytes 11524
  10.7 96.1 %copy-start.38 = (f32[256,32]{0,1:T(8,128)}, f32[256,32]{0,1:T(8,128)S(1)}, u32[]{:S(2)}) copy-start(f32[256,32]{0,1:T(8,128)S(1)} %get-tuple-element.95) | copy-start | bytes 98308
  10.8 96.1 %copy-start.40 = (f32[256,32]{0,1:T(8,128)}, f32[256,32]{0,1:T(8,128)S(1)}, u32[]{:S(2)}) copy-start(f32[256,32]{0,1:T(8,128)S(1)} %get-tuple-element.96) | copy-start | bytes 98308
  87.7 50.7 %all-gather.12.cloned.1.call-start = ((), (), s32[]{:S(2)}) async-start(), calls=%async_computation.12 | async-start | bytes 1638400 | tf_op jit(solution)/shard_map/all_gather | solution.py:136
  88.5 77.4 %all-gather.18.cloned.1.call-start = ((), (), s32[]{:S(2)}) async-start(), calls=%async_computation.15 | async-start | bytes 1638400 | tf_op jit(solution)/shard_map/all_gather | solution.py:137
  90.5 93.2 %all-gather.10.cloned.1.call-start = ((), (), s32[]{:S(2)}) async-start(), calls=%async_computation.11 | async-start | bytes 1638400 | tf_op jit(solution)/shard_map/all_gather | solution.py:137
  92.4 161.9 %all-gather.14.cloned.1.call-start = ((), (), s32[]{:S(2)}) async-start(), calls=%async_computation.13 | async-start | bytes 10813440 | tf_op jit(solution)/shard_map/all_gather | solution.py:118
  93.0 228.0 %all-gather.16.cloned.1.call-start = ((), (), s32[]{:S(2)}) async-start(), calls=%async_computation.14 | async-start | bytes 5406720 | tf_op jit(solution)/shard_map/all_gather | solution.py:119
  93.7 564.2 %reduce-scatter.9.cloned.1.call-start = ((), (), s32[]{:S(2)}) async-start(), calls=%async_computation.19 | async-start | bytes 1638400 | tf_op jit(solution)/shard_map/reduce_scatter | solution.py:220
  110.5 15.0 %copy-start.21 = (bf16[2,256,15,32]{1,3,2,0:T(8,128)(2,1)}, bf16[2,256,15,32]{1,3,2,0:T(8,128)(2,1)S(1)}, u32[]{:S(2)}) copy-start(bf16[2,256,15,32]{1,3,2,0:T(8,128)(2,1)S(1)} %get-tuple-element.66) | copy-start | bytes 1474564
  110.5 28.0 %copy-start.18 = (bf16[2,256,15,32]{1,3,2,0:T(8,128)(2,1)}, bf16[2,256,15,32]{1,3,2,0:T(8,128)(2,1)S(1)}, u32[]{:S(2)}) copy-start(bf16[2,256,15,32]{1,3,2,0:T(8,128)(2,1)S(1)} %get-tuple-element.48) | copy-start | bytes 1474564
  110.5 28.0 %copy-start.20 = (bf16[2,256,15,32]{1,3,2,0:T(8,128)(2,1)}, bf16[2,256,15,32]{1,3,2,0:T(8,128)(2,1)S(1)}, u32[]{:S(2)}) copy-start(bf16[2,256,15,32]{1,3,2,0:T(8,128)(2,1)S(1)} %get-tuple-element.49) | copy-start | bytes 1474564
  203.0 187.0 %copy-start.53 = (f32[2,256]{1,0:T(2,128)}, f32[2,256]{1,0:T(2,128)S(1)}, u32[]{:S(2)}) copy-start(f32[2,256]{1,0:T(2,128)S(1)} %get-tuple-element.91) | copy-start | bytes 6148
  203.0 187.0 %copy-start.55 = (f32[2,256]{1,0:T(2,128)}, f32[2,256]{1,0:T(2,128)S(1)}, u32[]{:S(2)}) copy-start(f32[2,256]{1,0:T(2,128)S(1)} %get-tuple-element.92) | copy-start | bytes 6148
  203.0 187.0 %copy-start.57 = (f32[2,256]{1,0:T(2,128)}, f32[2,256]{1,0:T(2,128)S(1)}, u32[]{:S(2)}) copy-start(f32[2,256]{1,0:T(2,128)S(1)} %get-tuple-element.89) | copy-start | bytes 6148
  203.0 187.0 %copy-start.59 = (f32[2,256]{1,0:T(2,128)}, f32[2,256]{1,0:T(2,128)S(1)}, u32[]{:S(2)}) copy-start(f32[2,256]{1,0:T(2,128)S(1)} %get-tuple-element.90) | copy-start | bytes 6148
  329.1 21.8 %slice-start = ((s8[10485760]{0:T(1024)(128)(4,1)}), s8[4194304]{0:T(1024)(128)(4,1)S(1)}, s32[]{:S(2)}) async-start(s8[10485760]{0:T(1024)(128)(4,1)} %bitcast.340), calls=%async_computation.21 | async-start | bytes 8388608
  329.1 21.8 %slice-start.1 = ((s8[10485760]{0:T(1024)(128)(4,1)}), s8[4194304]{0:T(1024)(128)(4,1)S(1)}, s32[]{:S(2)}) async-start(s8[10485760]{0:T(1024)(128)(4,1)} %bitcast.340), calls=%async_computation.22 | async-start | bytes 8388608
  375.0 15.0 %copy-start.3 = (f32[2,256,960]{1,2,0:T(8,128)S(1)}, f32[2,256,960]{1,2,0:T(8,128)}, u32[]{:S(2)}) copy-start(f32[2,256,960]{1,2,0:T(8,128)} %copy-done.2) | copy-start | bytes 5898244
  399.1 24.2 %copy-start.9 = (bf16[2,256,960]{1,2,0:T(8,128)(2,1)}, bf16[2,256,960]{1,2,0:T(8,128)(2,1)S(1)}, u32[]{:S(2)}) copy-start(bf16[2,256,960]{1,2,0:T(8,128)(2,1)S(1)} %convolution_convert_fusion) | copy-start | bytes 2949124
  423.3 26.8 %copy-start.22 = (bf16[2,256,15,32]{1,3,2,0:T(8,128)(2,1)S(1)}, bf16[2,256,15,32]{1,3,2,0:T(8,128)(2,1)}, u32[]{:S(2)}) copy-start(bf16[2,256,15,32]{1,3,2,0:T(8,128)(2,1)} %copy-done.21) | copy-start | bytes 1474564
  423.3 26.8 %copy-start.23 = (bf16[2,256,15,32]{1,3,2,0:T(8,128)(2,1)S(1)}, bf16[2,256,15,32]{1,3,2,0:T(8,128)(2,1)}, u32[]{:S(2)}) copy-start(bf16[2,256,15,32]{1,3,2,0:T(8,128)(2,1)} %get-tuple-element.67) | copy-start | bytes 1474564
  461.5 198.3 %reduce-scatter.5.cloned.1.call-start = ((), (), s32[]{:S(2)}) async-start(), calls=%async_computation.17 | async-start | bytes 1638400 | tf_op jit(solution)/shard_map/reduce_scatter | solution.py:220
  489.1 26.6 %copy-start.19 = (bf16[2,256,15,32]{1,3,2,0:T(8,128)(2,1)S(1)}, bf16[2,256,15,32]{1,3,2,0:T(8,128)(2,1)}, u32[]{:S(2)}) copy-start(bf16[2,256,15,32]{1,3,2,0:T(8,128)(2,1)} %copy-done.18) | copy-start | bytes 1474564
  527.3 136.5 %reduce-scatter.11.cloned.1.call-start = ((), (), s32[]{:S(2)}) async-start(), calls=%async_computation.20 | async-start | bytes 1638400 | tf_op jit(solution)/shard_map/reduce_scatter | solution.py:223
  564.9 78.5 %all-to-all-start.4 = ((bf16[960,8,4,80]{0,3,1,2:T(8,128)(2,1)}), bf16[960,8,4,80]{0,3,1,2:T(8,128)(2,1)}, u32[]{:S(2)}, u32[]{:S(2)}) async-start(bf16[960,8,4,80]{0,3,1,2:T(8,128)(2,1)} %copy.67), calls=%async_computation.8 | async-start | bytes 10485760 | tf_op jit(solution)/shard_map/all_to_all | solution.py:263
  570.0 99.9 %reduce-scatter.7.cloned.1.call-start = ((), (), s32[]{:S(2)}) async-start(), calls=%async_computation.18 | async-start | bytes 1638400 | tf_op jit(solution)/shard_map/reduce_scatter | solution.py:223
  648.7 46.1 %all-to-all-start.5 = ((bf16[960,8,80]{0,2,1:T(8,128)(2,1)}), bf16[960,8,80]{0,2,1:T(8,128)(2,1)S(1)}, u32[]{:S(2)}, u32[]{:S(2)}) async-start(bf16[960,8,80]{0,2,1:T(8,128)(2,1)} %reduce_sum.273), calls=%async_computation.9 | async-start | bytes 2621440 | tf_op jit(solution)/shard_map/all_to_all | solution.py:277
  694.8 64.7 %all-to-all-start = ((bf16[960,8,4,80]{0,3,1,2:T(8,128)(2,1)}), bf16[960,8,4,80]{0,3,1,2:T(8,128)(2,1)}, u32[]{:S(2)}, u32[]{:S(2)}) async-start(bf16[960,8,4,80]{0,3,1,2:T(8,128)(2,1)} %copy.62), calls=%async_computation.4 | async-start | bytes 10485760 | tf_op jit(solution)/shard_map/all_to_all | solution.py:249
  759.5 121.6 %all-to-all-start.2 = ((bf16[960,8,4,160]{0,3,1,2:T(8,128)(2,1)}), bf16[960,8,4,160]{0,3,1,2:T(8,128)(2,1)}, u32[]{:S(2)}, u32[]{:S(2)}) async-start(bf16[960,8,4,160]{0,3,1,2:T(8,128)(2,1)} %copy.64), calls=%async_computation.6 | async-start | bytes 20971520 | tf_op jit(solution)/shard_map/all_to_all | solution.py:256
  777.0 110.3 %copy-start.70 = (s32[4,256]{1,0:T(4,128)S(1)}, s32[4,256]{1,0:T(4,128)}, u32[]{:S(2)}) copy-start(s32[4,256]{1,0:T(4,128)} %param.11) | copy-start | bytes 12292
  881.0 37.4 %all-to-all-start.1 = ((bf16[8,960,1,80]{1,3,2,0:T(8,128)(2,1)}), bf16[8,960,1,80]{1,3,2,0:T(8,128)(2,1)}, u32[]{:S(2)}, u32[]{:S(2)}) async-start(bf16[8,960,1,80]{1,3,2,0:T(8,128)(2,1)} %fusion.105), calls=%async_computation.5 | async-start | bytes 2621440 | tf_op jit(solution)/shard_map/all_to_all | solution.py:74
  897.2 25.7 %copy-start.52 = (f32[4,256]{1,0:T(4,128)S(1)}, f32[4,256]{1,0:T(4,128)}, u32[]{:S(2)}) copy-start(f32[4,256]{1,0:T(4,128)} %copy-done.51) | copy-start | bytes 12292
  897.2 25.7 %copy-start.66 = (f32[1,2,256]{2,0,1:T(1,128)S(1)}, f32[1,2,256]{2,0,1:T(1,128)}, u32[]{:S(2)}) copy-start(f32[1,2,256]{2,0,1:T(1,128)} %copy-done.65) | copy-start | bytes 6148
  897.2 25.7 %copy-start.68 = (f32[1,2,256]{2,0,1:T(1,128)S(1)}, f32[1,2,256]{2,0,1:T(1,128)}, u32[]{:S(2)}) copy-start(f32[1,2,256]{2,0,1:T(1,128)} %copy-done.67) | copy-start | bytes 6148
  897.2 25.8 %copy-start.84 = (f32[2,256]{1,0:T(2,128)S(1)}, f32[2,256]{1,0:T(2,128)}, u32[]{:S(2)}) copy-start(f32[2,256]{1,0:T(2,128)} %get-tuple-element.20) | copy-start | bytes 6148
  897.2 25.8 %copy-start.85 = (f32[2,256]{1,0:T(2,128)S(1)}, f32[2,256]{1,0:T(2,128)}, u32[]{:S(2)}) copy-start(f32[2,256]{1,0:T(2,128)} %get-tuple-element.42) | copy-start | bytes 6148
  918.4 97.5 %all-to-all-start.3 = ((bf16[960,8,160]{0,2,1:T(8,128)(2,1)}), bf16[960,8,160]{0,2,1:T(8,128)(2,1)}, u32[]{:S(2)}, u32[]{:S(2)}) async-start(bf16[960,8,160]{0,2,1:T(8,128)(2,1)} %reduce_sum.271), calls=%async_computation.7 | async-start | bytes 5242880 | tf_op jit(solution)/shard_map/all_to_all | solution.py:274
  936.6 66.7 %copy-start.47 = (f32[960]{0:T(1024)S(1)}, f32[960]{0:T(1024)}, u32[]{:S(2)}) copy-start(f32[960]{0:T(1024)} %param.17) | copy-start | bytes 11524
  936.6 66.7 %copy-start.58 = (f32[2,256]{1,0:T(2,128)S(1)}, f32[2,256]{1,0:T(2,128)}, u32[]{:S(2)}) copy-start(f32[2,256]{1,0:T(2,128)} %copy-done.57) | copy-start | bytes 6148
  936.6 66.7 %copy-start.64 = (f32[2,256]{1,0:T(2,128)S(1)}, f32[2,256]{1,0:T(2,128)}, u32[]{:S(2)}) copy-start(f32[2,256]{1,0:T(2,128)} %copy-done.63) | copy-start | bytes 6148
  936.6 66.7 %copy-start.74 = (f32[2,256]{1,0:T(2,128)S(1)}, f32[2,256]{1,0:T(2,128)}, u32[]{:S(2)}) copy-start(f32[2,256]{1,0:T(2,128)} %get-tuple-element.87) | copy-start | bytes 6148
  (70 other events, 384.9 us)
Sparse Core Ops, SparseCore 0:
  10.8 68.0 all-gather.7
  87.8 16.8 all-gather.19
  106.9 18.3 all-gather.11
  127.2 18.3 all-gather.17
  146.9 18.3 all-gather.9
  168.0 86.2 all-gather.13
  257.1 63.8 all-gather.15
  461.7 24.9 reduce-scatter.8
  527.4 24.9 reduce-scatter.4
  555.3 33.5 reduce-scatter.10
  591.5 33.5 reduce-scatter.6
